TPU v7x, 256 devices: a whole 4x4x8 slice. The times are simulated.
256 devices in a mesh: gx: 8 (over z), gy: 8 (over x, core), gz: 4 (over y).
Axes of the slice: x: 4, y: 4, z: 8, core: 2. Of those that a mesh axis runs over, the one named last changes fastest.
Arguments:
- velocity: float32 [3, 64, 128, 1024], P(None, 'gz', 'gx', 'gy'), may hold values from -20 to 20
- owner: int32 [262144, 1], P(('gx', 'gy', 'gz')), may hold values from 0 to 63; in each aligned block of 1024 rows (0 to 1023, 1024 to 2047, ...) at most 64 rows name the same one
- cell_x: int32 [262144], P(('gx', 'gy', 'gz')), may hold values from 0 to 14
- cell_y: int32 [262144], P(('gx', 'gy', 'gz')), may hold values from 0 to 126
- cell_z: int32 [262144], P(('gx', 'gy', 'gz')), may hold values from 0 to 14
- query_weights: float32 [3, 262144], P(None, ('gx', 'gy', 'gz')), may hold values from 0 to 1
Outputs:
- query_stress: float32 [6, 262144], P(None, ('gx', 'gy', 'gz'))
Inputs may be any that keep to these rules, and one draw needn't show every extreme that they name: Among the queries held by one device, at most 64 name the same owner, and in every draw some owner is named by exactly 64 of them. `cell_x`: the corner cell plus one stays in the same brick.
All inputs are finite; a program needn't handle non-finite values.
Results may differ from a plain program's by a relative error of at most 0.0003.
Values sent between devices are 32-bit elements; how exact they have to be, the bound alone decides.
A program may use at most 64 MiB of HBM per device.

v0:
```python
import jax
import jax.numpy as jnp
from jax import lax
from jax.sharding import PartitionSpec as P

FW = 32
PAIRS = ((0, 0), (0, 1), (0, 2), (1, 1), (1, 2), (2, 2))


def padded(x, sides, width):
    for axis, dim in sides:
        devices, length = (lax.axis_size(axis), x.shape[dim])
        up = [(i, (i + 1) % devices) for i in range(devices)]
        down = [(j, i) for i, j in up]
        last = lax.slice_in_dim(x, length - width, length, axis=dim)
        initial = lax.slice_in_dim(x, 0, width, axis=dim)
        before = lax.ppermute(last, axis, up)
        after = lax.ppermute(initial, axis, down)
        x = jnp.concatenate([before, x, after], axis=dim)
    return x


def taps(radius, width):
    offsets = jnp.arange(2 * radius + 1).astype(jnp.float32) - radius
    values = jnp.exp(-6.0 * offsets * offsets / (width * width))
    return values / jnp.sum(values)


def band(length, radius, width):
    weights = taps(radius, width)
    rows = jnp.arange(length + 2 * radius)[:, None]
    cols = jnp.arange(length)[None, :]
    offset = rows - cols
    inside = (offset >= 0) & (offset <= 2 * radius)
    picked = weights[jnp.clip(offset, 0, 2 * radius)]
    return jnp.where(inside, picked, jnp.zeros_like(picked))


def filter_x(fields, matrix):
    return jnp.einsum("czpy,pq->czqy", fields, matrix, precision=lax.Precision.HIGHEST)


def filter_y(fields, matrix):
    return jnp.einsum("czxp,pq->czxq", fields, matrix, precision=lax.Precision.HIGHEST)


def interpolate(flat_stress, index, weight, size_x, size_y):
    shape = index.shape[1:]
    base = index[0].reshape(-1)
    offsets = weight.reshape(3, -1)
    wx = offsets[0]
    wy = offsets[1]
    wz = offsets[2]
    total = jnp.zeros((6, base.shape[0]), jnp.float32)
    for dz in (0, 1):
        for dx in (0, 1):
            for dy in (0, 1):
                corner = base + dz * size_x * size_y + dx * size_y + dy
                values = jnp.take(flat_stress, corner, axis=1)
                term = (
                    (wz if dz else 1.0 - wz) * (wx if dx else 1.0 - wx) * (wy if dy else 1.0 - wy)
                )
                total = total + term[None, :] * values
    return total.reshape((6,) + shape)


def on_device(velocity, owner, cell_x, cell_y, cell_z, query_weights):
    radius = FW // 2
    size_z = velocity.shape[1]
    size_x = velocity.shape[2]
    size_y = velocity.shape[3]
    layered = padded(velocity, (("gz", 1),), radius)
    band_z = band(size_z, radius, FW)
    band_x = band(size_x, radius, FW)
    band_y = band(size_y, radius, FW)
    fields = []
    for comp in range(3):
        fields.append(
            jnp.einsum("pxy,pz->zxy", layered[comp], band_z, precision=lax.Precision.HIGHEST)
        )
    for first, second in PAIRS:
        product = layered[first] * layered[second]
        fields.append(jnp.einsum("pxy,pz->zxy", product, band_z, precision=lax.Precision.HIGHEST))
    stacked = jnp.stack(fields)
    margined = padded(stacked, (("gx", 2), ("gy", 3)), radius)
    filtered = filter_y(filter_x(margined, band_x), band_y)
    stress = jnp.stack(
        [
            filtered[3 + k] - filtered[first] * filtered[second]
            for k, (first, second) in enumerate(PAIRS)
        ]
    )
    flat_stress = stress.reshape(6, -1)
    bricks_x = lax.axis_size("gx")
    bricks_y = lax.axis_size("gy")
    owners = bricks_x * bricks_y
    count = owner.shape[0]
    capacity = 4 * count // owners
    target = owner[:, 0]
    order = jnp.argsort(target, stable=True)
    sorted_target = target[order]
    tally = jnp.sum(
        (target[:, None] == jnp.arange(owners, dtype=jnp.int32)[None, :]).astype(jnp.int32), axis=0
    )
    starts = jnp.cumsum(tally) - tally
    sorted_rank = jnp.arange(count, dtype=jnp.int32) - starts[sorted_target]
    rank = jnp.zeros((count,), jnp.int32).at[order].set(sorted_rank)
    slot = target * capacity + rank
    local_cell = (cell_z * size_x + cell_x) * size_y + cell_y
    send_index = jnp.zeros((owners * capacity,), jnp.int32).at[slot].set(local_cell)
    send_weight = jnp.zeros((3, owners * capacity), jnp.float32).at[:, slot].set(query_weights)
    values = interpolate(
        flat_stress,
        lax.all_to_all(
            send_index.reshape(1, owners, capacity),
            ("gx", "gy"),
            split_axis=1,
            concat_axis=1,
            tiled=True,
        ),
        lax.all_to_all(
            send_weight.reshape(3, owners, capacity),
            ("gx", "gy"),
            split_axis=1,
            concat_axis=1,
            tiled=True,
        ),
        size_x,
        size_y,
    )
    returned = lax.all_to_all(values, ("gx", "gy"), split_axis=1, concat_axis=1, tiled=True)
    flat_back = returned.reshape(6, owners * capacity)
    return jnp.take(flat_back, slot, axis=1)


def solution(mesh):
    placed = (
        P(None, "gz", "gx", "gy"),
        P(("gx", "gy", "gz"), None),
        P(("gx", "gy", "gz")),
        P(("gx", "gy", "gz")),
        P(("gx", "gy", "gz")),
        P(None, ("gx", "gy", "gz")),
    )
    return jax.shard_map(
        on_device,
        mesh=mesh,
        in_specs=placed,
        out_specs=P(None, ("gx", "gy", "gz")),
        check_vma=False,
    )
```

profile of v0, /device:TPU:1, one launch (start us, length us, event | category | flops | bytes accessed | tf_op | source)
XLA Modules:
  0.0 546.4 jit_solution(7970189455837514659)
XLA Ops:
  1.1 2.2 collective-permute-start
  7.4 5.1 sort.17
  12.6 4.5 gather_fusion
  17.1 4.3 compare_select_fusion.11
  24.9 4.8 gather_fusion.1
  33.3 5.7 %collective-permute-start.3 = (f32[9,16,16,128]{3,1,2,0:T(8,128)S(1)}, f32[9,16,16,128]{3,1,2,0:T(8,128)}, u32[]{:S(2)}, u32[]{:S(2)}) collective-permute-start(f32[9,16,16,128]{3,1,2,0:T(8,128)S(1)} %fusion.4), channel_id=1, source_target_pairs={{32,0},{64,32},{96,64},{128,96},{160,128},{192,160},{224,192},{0,2... | collective-permute-start | bytes 3538952 | tf_op jit(solution)/shard_map/ppermute | solution.py:18
  38.9 35.9 %select_subtract_fusion = s32[1024]{0:T(1024)S(1)} fusion(pred[1024]{0:T(1024)(128)(4,1)S(1)} %get-tuple-element.67, pred[1024]{0:T(1024)(128)(4,1)S(1)} %get-tuple-element.66, pred[1024]{0:T(1024)(128)(4,1)S(1)} %get-tuple-element.65, pred[1024]{0:T(1024)(128)(4,1)S(1)} %get-tuple-element.64, pred[1024]{0:T(1024)(128)(4,1)S(1)} %get-tuple-element.63, ...), kind=kLoop, calls=%fused_computation.212 | loop fusion | flops 59392 | bytes 66788 | tf_op jit(solution)/shard_map/sub | solution.py:106
  74.9 4.3 scatter_custom_fusion
  79.8 4.3 scatter_custom_fusion.2
  84.9 9.6 %all-to-all-start.1 = ((s32[1,64,64]{2,0,1:T(1,128)}), s32[1,64,64]{2,0,1:T(1,128)S(1)}, u32[]{:S(2)}, u32[]{:S(2)}) async-start(s32[1,64,64]{2,0,1:T(1,128)} %reshape.232), calls=%async_computation.1 | async-start | bytes 65536 | tf_op jit(solution)/shard_map/all_to_all | solution.py:114
  94.5 209.5 %gather_fusion.2 = f32[20480]{0:T(1024)} fusion(f32[33]{0:T(128)S(1)} %broadcast_divide_fusion, s32[20480]{0:T(1024)S(1)} %fusion.29), kind=kCustom, calls=%fused_computation.10 | custom fusion | bytes 245760 | tf_op jit(solution)/shard_map/gather | solution.py:35
  305.0 4.0 scatter_custom_fusion.1
  310.5 10.5 %all-to-all-start = ((f32[64,1,192]{2,1,0:T(1,128)}), f32[64,1,192]{2,1,0:T(1,128)}, u32[]{:S(2)}, u32[]{:S(2)}) async-start(f32[64,1,192]{2,1,0:T(1,128)} %reshape.699), calls=%async_computation | async-start | bytes 131072 | tf_op jit(solution)/shard_map/all_to_all | solution.py:121
  324.8 2.9 fusion.84
  327.8 3.3 copy.121
  339.9 7.4 %collective-permute-done.5 = f32[9,16,48,16]{2,3,1,0:T(8,128)} collective-permute-done((f32[9,16,48,16]{2,3,1,0:T(8,128)}, f32[9,16,48,16]{2,3,1,0:T(8,128)}, u32[]{:S(2)}, u32[]{:S(2)}) %collective-permute-start.5) | collective-permute-done | bytes 442400 | tf_op jit(solution)/shard_map/ppermute | solution.py:18
  347.4 2.3 copy.123
  349.7 3.4 copy.122
  353.1 6.5 %pad_maximum_fusion = f32[9,16,48,160]{3,1,2,0:T(8,128)S(1)} fusion(f32[9,16,48,16]{3,1,2,0:T(8,128)S(1)} %copy.123, f32[9,16,16,128]{3,1,2,0:T(8,128)} %collective-permute-done.3, f32[9,16,16,128]{3,1,2,0:T(8,128)} %copy-done.1, f32[9,16,16,128]{3,1,2,0:T(8,128)} %collective-permute-done.2, f32[9,16,48,16]{3,1,2,0:T(8,128)} %copy.122), kind=kLoop, calls=%fused_computation.15 | loop fusion | flops 4423680 | bytes 8847360 | tf_op jit(solution)/shard_map/concatenate | solution.py:19
  359.7 7.4 %fusion = f32[16,9,16,160]{3,0,2,1:T(8,128)S(1)} fusion(f32[9,16,48,160]{3,1,2,0:T(8,128)S(1)} %pad_maximum_fusion, f32[48,16]{1,0:T(8,128)S(1)} %copy-done.3), kind=kOutput, calls=%fused_computation.16 | convolution fusion | flops 212340480 | bytes 5901312 | tf_op jit(solution)/shard_map/czpy,pq->czqy/dot_general | solution.py:40
  370.5 9.0 %copy.126 = f32[6,32768]{0,1:T(8,128)} copy(f32[6,32768]{1,0:T(8,128)S(1)} %stack.67) | data formatting | bytes 1572864 | tf_op jit(solution)/shard_map/stack | solution.py:87
  379.5 16.6 %gather_fusion.11 = f32[4096,6]{1,0:T(8,128)S(1)} fusion(f32[6,32768]{0,1:T(8,128)} %copy.126, s32[4096]{0:T(1024)S(1)} %copy-done.14), kind=kCustom, calls=%fused_computation.7.clone | custom fusion | bytes 212992 | tf_op jit(solution)/shard_map/jit(_take)/gather | solution.py:59
  396.7 16.6 %gather_fusion.10 = f32[4096,6]{1,0:T(8,128)S(1)} fusion(f32[6,32768]{0,1:T(8,128)} %copy.126, s32[4096]{0:T(1024)S(1)} %copy-done.13), kind=kCustom, calls=%fused_computation.6.clone | custom fusion | bytes 212992 | tf_op jit(solution)/shard_map/jit(_take)/gather | solution.py:59
  414.0 16.8 %gather_fusion.9 = f32[4096,6]{1,0:T(8,128)S(1)} fusion(f32[6,32768]{0,1:T(8,128)} %copy.126, s32[4096]{0:T(1024)S(1)} %copy-done.12), kind=kCustom, calls=%fused_computation.5.clone | custom fusion | bytes 212992 | tf_op jit(solution)/shard_map/jit(_take)/gather | solution.py:59
  431.4 16.6 %gather_fusion.8 = f32[4096,6]{1,0:T(8,128)S(1)} fusion(f32[6,32768]{0,1:T(8,128)} %copy.126, s32[4096]{0:T(1024)S(1)} %copy-done.11), kind=kCustom, calls=%fused_computation.4.clone | custom fusion | bytes 212992 | tf_op jit(solution)/shard_map/jit(_take)/gather | solution.py:59
  448.6 16.6 %gather_fusion.7 = f32[4096,6]{1,0:T(8,128)S(1)} fusion(f32[6,32768]{0,1:T(8,128)} %copy.126, s32[4096]{0:T(1024)S(1)} %copy-done.10), kind=kCustom, calls=%fused_computation.3.clone | custom fusion | bytes 212992 | tf_op jit(solution)/shard_map/jit(_take)/gather | solution.py:59
  465.8 16.6 %gather_fusion.6 = f32[4096,6]{1,0:T(8,128)S(1)} fusion(f32[6,32768]{0,1:T(8,128)} %copy.126, s32[4096]{0:T(1024)S(1)} %copy-done.9), kind=kCustom, calls=%fused_computation.2.clone | custom fusion | bytes 212992 | tf_op jit(solution)/shard_map/jit(_take)/gather | solution.py:59
  483.0 16.6 %gather_fusion.5 = f32[4096,6]{1,0:T(8,128)S(1)} fusion(f32[6,32768]{0,1:T(8,128)} %copy.126, s32[4096]{0:T(1024)S(1)} %copy-done.8), kind=kCustom, calls=%fused_computation.1.clone | custom fusion | bytes 212992 | tf_op jit(solution)/shard_map/jit(_take)/gather | solution.py:59
  500.3 16.6 %gather_fusion.4 = f32[4096,6]{1,0:T(8,128)S(1)} fusion(f32[6,32768]{0,1:T(8,128)} %copy.126, s32[4096]{0:T(1024)S(1)} %copy-done.7), kind=kCustom, calls=%fused_computation.clone | custom fusion | bytes 212992 | tf_op jit(solution)/shard_map/jit(_take)/gather | solution.py:59
  518.9 11.0 %all-to-all-start.2 = ((f32[64,1,384]{2,1,0:T(1,128)}), f32[64,1,384]{2,1,0:T(1,128)S(1)}, u32[]{:S(2)}, u32[]{:S(2)}) async-start(f32[64,1,384]{2,1,0:T(1,128)} %reshape.701), calls=%async_computation.2 | async-start | bytes 196608 | tf_op jit(solution)/shard_map/all_to_all | solution.py:131
  530.0 10.6 %all-to-all-done.2 = f32[64,1,384]{2,1,0:T(1,128)S(1)} async-done(((f32[64,1,384]{2,1,0:T(1,128)}), f32[64,1,384]{2,1,0:T(1,128)S(1)}, u32[]{:S(2)}, u32[]{:S(2)}) %all-to-all-start.2) | async-done | bytes 98336 | tf_op jit(solution)/shard_map/all_to_all | solution.py:131
  542.3 2.8 gather_fusion.3
  (152 shorter events, 41.1 us)
Async XLA Ops:
  1.1 28.6 %collective-permute-start = (f32[3,16,16,128]{3,1,2,0:T(8,128)S(1)}, f32[3,16,16,128]{3,1,2,0:T(8,128)S(1)}, u32[]{:S(2)}, u32[]{:S(2)}) collective-permute-start(f32[3,16,16,128]{3,1,2,0:T(8,128)S(1)} %copy.108), channel_id=1, source_target_pairs={{0,1},{1,2},{2,3},{3,0},{4,5},{5,6},{6,7},{7,4},{8,9},{9,10},{10,1... | collective-permute-start | bytes 1179656 | tf_op jit(solution)/shard_map/ppermute | solution.py:17
  3.3 26.6 %collective-permute-start.1 = (f32[3,16,16,128]{3,1,2,0:T(8,128)S(1)}, f32[3,16,16,128]{3,1,2,0:T(8,128)S(1)}, u32[]{:S(2)}, u32[]{:S(2)}) collective-permute-start(f32[3,16,16,128]{3,1,2,0:T(8,128)S(1)} %copy.108), channel_id=1, source_target_pairs={{1,0},{2,1},{3,2},{0,3},{5,4},{6,5},{7,6},{4,7},{9,8},{10,9},{11,1... | collective-permute-start | bytes 1179656 | tf_op jit(solution)/shard_map/ppermute | solution.py:18
  30.7 49.1 %copy-start.31 = (s32[1024]{0:T(1024)S(1)}, s32[1024]{0:T(1024)}, u32[]{:S(2)}) copy-start(s32[1024]{0:T(1024)} %param.11) | copy-start | bytes 12292
  30.7 49.1 %copy-start.32 = (s32[1024]{0:T(1024)S(1)}, s32[1024]{0:T(1024)}, u32[]{:S(2)}) copy-start(s32[1024]{0:T(1024)} %param.10) | copy-start | bytes 12292
  30.7 49.1 %copy-start.33 = (s32[1024]{0:T(1024)S(1)}, s32[1024]{0:T(1024)}, u32[]{:S(2)}) copy-start(s32[1024]{0:T(1024)} %param.12) | copy-start | bytes 12292
  33.3 289.7 %copy-start.1 = (f32[9,16,16,128]{3,1,2,0:T(8,128)}, f32[9,16,16,128]{3,1,2,0:T(8,128)S(1)}, u32[]{:S(2)}) copy-start(f32[9,16,16,128]{3,1,2,0:T(8,128)S(1)} %fusion.4) | copy-start | bytes 3538948
  33.3 289.7 %collective-permute-start.3 = (f32[9,16,16,128]{3,1,2,0:T(8,128)S(1)}, f32[9,16,16,128]{3,1,2,0:T(8,128)}, u32[]{:S(2)}, u32[]{:S(2)}) collective-permute-start(f32[9,16,16,128]{3,1,2,0:T(8,128)S(1)} %fusion.4), channel_id=1, source_target_pairs={{32,0},{64,32},{96,64},{128,96},{160,128},{192,160},{224,192},{0,2... | collective-permute-start | bytes 3538952 | tf_op jit(solution)/shard_map/ppermute | solution.py:18
  38.9 284.0 %collective-permute-start.2 = (f32[9,16,16,128]{3,1,2,0:T(8,128)S(1)}, f32[9,16,16,128]{3,1,2,0:T(8,128)}, u32[]{:S(2)}, u32[]{:S(2)}) collective-permute-start(f32[9,16,16,128]{3,1,2,0:T(8,128)S(1)} %fusion.4), channel_id=1, source_target_pairs={{0,32},{32,64},{64,96},{96,128},{128,160},{160,192},{192,224},{224... | collective-permute-start | bytes 3538952 | tf_op jit(solution)/shard_map/ppermute | solution.py:17
  79.8 225.2 %copy-start.28 = (s32[1024]{0:T(1024)}, s32[1024]{0:T(1024)S(1)}, u32[]{:S(2)}) copy-start(s32[1024]{0:T(1024)S(1)} %get-tuple-element.69) | copy-start | bytes 12292
  84.9 225.6 %all-to-all-start.1 = ((s32[1,64,64]{2,0,1:T(1,128)}), s32[1,64,64]{2,0,1:T(1,128)S(1)}, u32[]{:S(2)}, u32[]{:S(2)}) async-start(s32[1,64,64]{2,0,1:T(1,128)} %reshape.232), calls=%async_computation.1 | async-start | bytes 65536 | tf_op jit(solution)/shard_map/all_to_all | solution.py:114
  94.5 209.5 %copy-start.27 = (f32[3,1024]{1,0:T(4,128)S(1)}, f32[3,1024]{1,0:T(4,128)}, u32[]{:S(2)}) copy-start(f32[3,1024]{1,0:T(4,128)} %param.13) | copy-start | bytes 36868
  310.5 25.9 %all-to-all-start = ((f32[64,1,192]{2,1,0:T(1,128)}), f32[64,1,192]{2,1,0:T(1,128)}, u32[]{:S(2)}, u32[]{:S(2)}) async-start(f32[64,1,192]{2,1,0:T(1,128)} %reshape.699), calls=%async_computation | async-start | bytes 131072 | tf_op jit(solution)/shard_map/all_to_all | solution.py:121
  331.1 16.2 %collective-permute-start.5 = (f32[9,16,48,16]{2,3,1,0:T(8,128)}, f32[9,16,48,16]{2,3,1,0:T(8,128)}, u32[]{:S(2)}, u32[]{:S(2)}) collective-permute-start(f32[9,16,48,16]{2,3,1,0:T(8,128)} %copy.121), channel_id=1, source_target_pairs={{4,0},{8,4},{12,8},{16,12},{20,16},{24,20},{28,24},{0,28},{5,1},{9... | collective-permute-start | bytes 1327112 | tf_op jit(solution)/shard_map/ppermute | solution.py:18
  333.8 15.9 %collective-permute-start.4 = (f32[9,16,48,16]{2,3,1,0:T(8,128)}, f32[9,16,48,16]{2,3,1,0:T(8,128)}, u32[]{:S(2)}, u32[]{:S(2)}) collective-permute-start(f32[9,16,48,16]{2,3,1,0:T(8,128)} %copy.120), channel_id=1, source_target_pairs={{0,4},{4,8},{8,12},{12,16},{16,20},{20,24},{24,28},{28,0},{1,5},{5... | collective-permute-start | bytes 1327112 | tf_op jit(solution)/shard_map/ppermute | solution.py:17
  396.7 17.2 %copy-start.12 = (s32[4096]{0:T(1024)S(1)}, s32[4096]{0:T(1024)}, u32[]{:S(2)}) copy-start(s32[4096]{0:T(1024)} %get-tuple-element.97) | copy-start | bytes 49156
  413.9 17.4 %copy-start.11 = (s32[4096]{0:T(1024)S(1)}, s32[4096]{0:T(1024)}, u32[]{:S(2)}) copy-start(s32[4096]{0:T(1024)} %get-tuple-element.98) | copy-start | bytes 49156
  431.4 17.2 %copy-start.10 = (s32[4096]{0:T(1024)S(1)}, s32[4096]{0:T(1024)}, u32[]{:S(2)}) copy-start(s32[4096]{0:T(1024)} %get-tuple-element.99) | copy-start | bytes 49156
  483.0 17.3 %copy-start.7 = (s32[4096]{0:T(1024)S(1)}, s32[4096]{0:T(1024)}, u32[]{:S(2)}) copy-start(s32[4096]{0:T(1024)} %get-tuple-element.96) | copy-start | bytes 49156
  500.2 17.3 %copy-start.15 = (f32[4096]{0:T(1024)S(1)}, f32[4096]{0:T(1024)}, u32[]{:S(2)}) copy-start(f32[4096]{0:T(1024)} %get-tuple-element.80) | copy-start | bytes 49156
  500.2 17.3 %copy-start.16 = (f32[4096]{0:T(1024)S(1)}, f32[4096]{0:T(1024)}, u32[]{:S(2)}) copy-start(f32[4096]{0:T(1024)} %get-tuple-element.81) | copy-start | bytes 49156
  500.2 17.4 %copy-start.17 = (f32[4096]{0:T(1024)S(1)}, f32[4096]{0:T(1024)}, u32[]{:S(2)}) copy-start(f32[4096]{0:T(1024)} %get-tuple-element.82) | copy-start | bytes 49156
  500.2 17.4 %copy-start.18 = (f32[4096]{0:T(1024)S(1)}, f32[4096]{0:T(1024)}, u32[]{:S(2)}) copy-start(f32[4096]{0:T(1024)} %get-tuple-element.83) | copy-start | bytes 49156
  500.2 17.4 %copy-start.19 = (f32[4096]{0:T(1024)S(1)}, f32[4096]{0:T(1024)}, u32[]{:S(2)}) copy-start(f32[4096]{0:T(1024)} %get-tuple-element.84) | copy-start | bytes 49156
  500.2 17.4 %copy-start.20 = (f32[4096]{0:T(1024)S(1)}, f32[4096]{0:T(1024)}, u32[]{:S(2)}) copy-start(f32[4096]{0:T(1024)} %get-tuple-element.85) | copy-start | bytes 49156
  500.3 17.4 %copy-start.21 = (f32[4096]{0:T(1024)S(1)}, f32[4096]{0:T(1024)}, u32[]{:S(2)}) copy-start(f32[4096]{0:T(1024)} %get-tuple-element.86) | copy-start | bytes 49156
  500.3 17.4 %copy-start.22 = (f32[4096]{0:T(1024)S(1)}, f32[4096]{0:T(1024)}, u32[]{:S(2)}) copy-start(f32[4096]{0:T(1024)} %get-tuple-element.87) | copy-start | bytes 49156
  500.3 17.4 %copy-start.23 = (pred[4096]{0:T(1024)(128)(4,1)S(1)}, pred[4096]{0:T(1024)(128)(4,1)}, u32[]{:S(2)}) copy-start(pred[4096]{0:T(1024)(128)(4,1)} %get-tuple-element.92) | copy-start | bytes 12292
  500.3 17.4 %copy-start.24 = (pred[4096]{0:T(1024)(128)(4,1)S(1)}, pred[4096]{0:T(1024)(128)(4,1)}, u32[]{:S(2)}) copy-start(pred[4096]{0:T(1024)(128)(4,1)} %get-tuple-element.93) | copy-start | bytes 12292
  500.3 17.4 %copy-start.25 = (pred[4096]{0:T(1024)(128)(4,1)S(1)}, pred[4096]{0:T(1024)(128)(4,1)}, u32[]{:S(2)}) copy-start(pred[4096]{0:T(1024)(128)(4,1)} %get-tuple-element.94) | copy-start | bytes 12292
  500.3 17.4 %copy-start.26 = (pred[4096]{0:T(1024)(128)(4,1)S(1)}, pred[4096]{0:T(1024)(128)(4,1)}, u32[]{:S(2)}) copy-start(pred[4096]{0:T(1024)(128)(4,1)} %get-tuple-element.95) | copy-start | bytes 12292
  518.0 27.2 %copy-start.30 = (pred[1024]{0:T(1024)(128)(4,1)S(1)}, pred[1024]{0:T(1024)(128)(4,1)}, u32[]{:S(2)}) copy-start(pred[1024]{0:T(1024)(128)(4,1)} %get-tuple-element.68) | copy-start | bytes 3076
  518.9 21.6 %all-to-all-start.2 = ((f32[64,1,384]{2,1,0:T(1,128)}), f32[64,1,384]{2,1,0:T(1,128)S(1)}, u32[]{:S(2)}, u32[]{:S(2)}) async-start(f32[64,1,384]{2,1,0:T(1,128)} %reshape.701), calls=%async_computation.2 | async-start | bytes 196608 | tf_op jit(solution)/shard_map/all_to_all | solution.py:131
  (11 other events, 109.0 us)
where the time goes:
time: 556 us; the launch traced here: 546 us
  local copies, waits for them, and re-layouts  409 us (74%)
  other arithmetic  63.9 us (11%)
  starting transfers between devices  42.2 us (8%)
  waiting for transfers between devices  18 us (3%)
  matrix products  12.6 us (2%)
    gather x3, local copies, waits for them, and re-layouts, band(): picked = weights[jnp.clip(offset, 0, 2 * radius)]  214 us
    gather x16, local copies, waits for them, and re-layouts, interpolate(): values = jnp.take(flat_stress, corner, axis=1)  138 us
    sub x1, other arithmetic, on_device(): sorted_rank = jnp.arange(count, dtype=jnp.int32) - starts[sorted_target]  35.9 us
  transfers between devices with their start and end apart: 9, of which 2 were waited for; matrix products, arithmetic and copies ran while one was open for 56% of the time, Pallas kernels for 0%

commit v1 on v0

--- a/solution.py
+++ b/solution.py
@@ -118,12 +118,18 @@
             concat_axis=1,
             tiled=True,
         ),
-        lax.all_to_all(
-            send_weight.reshape(3, owners, capacity),
-            ("gx", "gy"),
-            split_axis=1,
-            concat_axis=1,
-            tiled=True,
+        jnp.concatenate(
+            lax.all_to_all(
+                jnp.stack(
+                    jnp.split(
+                        send_weight.reshape(3, owners, capacity), lax.psum(1, ("gx", "gy")), axis=1
+                    )
+                ),
+                axis_name=("gx", "gy"),
+                split_axis=0,
+                concat_axis=0,
+            ),
+            axis=1,
         ),
         size_x,
         size_y,

time: 556 us -> 642 us (1.15)
  local copies, waits for them, and re-layouts: 409 us -> 490 us
    unnamed x76 -> x213, local copies, waits for them, and re-layouts: 4.19 us -> 82.2 us
  transfers between devices with their start and end apart: 9 -> 9, of which waited for: 2 -> 2; matrix products, arithmetic and copies ran while one was open for 56% -> 62% of each run, Pallas kernels for 0% -> 0%
where the time goes in v1:
time: 642 us; the launch traced here: 631 us
  local copies, waits for them, and re-layouts  490 us (76%)
  other arithmetic  66.1 us (10%)
  starting transfers between devices  41.8 us (7%)
  waiting for transfers between devices  19.4 us (3%)
  matrix products  12.6 us (2%)
    gather x3, local copies, waits for them, and re-layouts, band(): picked = weights[jnp.clip(offset, 0, 2 * radius)]  214 us
    gather x16, local copies, waits for them, and re-layouts, interpolate(): values = jnp.take(flat_stress, corner, axis=1)  138 us
    unnamed x213, local copies, waits for them, and re-layouts  82.2 us
    sub x1, other arithmetic, on_device(): sorted_rank = jnp.arange(count, dtype=jnp.int32) - starts[sorted_target]  35.7 us
  transfers between devices with their start and end apart: 9, of which 2 were waited for; matrix products, arithmetic and copies ran while one was open for 62% of the time, Pallas kernels for 0%

profile of v1, /device:TPU:1, one launch (start us, length us, event | category | flops | bytes accessed | tf_op | source)
XLA Modules:
  0.0 631.2 jit_solution(13335636742983576505)
XLA Ops:
  8.9 5.1 sort.17
  14.1 4.5 gather_fusion
  18.6 4.3 compare_select_fusion.11
  23.7 35.7 %select_subtract_fusion = s32[1024]{0:T(1024)S(1)} fusion(pred[1024]{0:T(1024)(128)(4,1)S(1)} %get-tuple-element.67, pred[1024]{0:T(1024)(128)(4,1)S(1)} %get-tuple-element.66, pred[1024]{0:T(1024)(128)(4,1)S(1)} %get-tuple-element.65, pred[1024]{0:T(1024)(128)(4,1)S(1)} %get-tuple-element.64, pred[1024]{0:T(1024)(128)(4,1)S(1)} %get-tuple-element.63, ...), kind=kLoop, calls=%fused_computation.276 | loop fusion | flops 59392 | bytes 66788 | tf_op jit(solution)/shard_map/sub | solution.py:106
  59.4 4.3 scatter_custom_fusion
  64.3 4.3 scatter_custom_fusion.2
  69.3 12.8 %all-to-all-start.1 = ((s32[1,64,64]{2,0,1:T(1,128)}), s32[1,64,64]{2,0,1:T(1,128)}, u32[]{:S(2)}, u32[]{:S(2)}) async-start(s32[1,64,64]{2,0,1:T(1,128)} %reshape.235), calls=%async_computation.1 | async-start | bytes 65536 | tf_op jit(solution)/shard_map/all_to_all | solution.py:114
  82.3 4.1 scatter_custom_fusion.1
  163.6 4.8 gather_fusion.1
  173.1 2.9 collective-permute-start.3
  178.4 209.6 %gather_fusion.2 = f32[20480]{0:T(1024)} fusion(f32[33]{0:T(128)S(1)} %broadcast_divide_fusion, s32[20480]{0:T(1024)} %fusion.29), kind=kCustom, calls=%fused_computation.10 | custom fusion | bytes 245760 | tf_op jit(solution)/shard_map/gather | solution.py:35
  388.6 2.4 reduce.131
  392.6 9.7 %all-to-all-start = ((f32[64,1,192]{2,1,0:T(1,128)}), f32[64,1,192]{2,1,0:T(1,128)}, u32[]{:S(2)}, u32[]{:S(2)}) async-start(f32[64,1,192]{2,1,0:T(1,128)} %reshape.702), calls=%async_computation | async-start | bytes 131072 | tf_op jit(solution)/shard_map/all_to_all | solution.py:122
  410.0 2.9 fusion.84
  412.9 3.3 copy.373
  423.7 8.8 %collective-permute-done.5 = f32[9,16,48,16]{2,3,1,0:T(8,128)} collective-permute-done((f32[9,16,48,16]{2,3,1,0:T(8,128)}, f32[9,16,48,16]{2,3,1,0:T(8,128)}, u32[]{:S(2)}, u32[]{:S(2)}) %collective-permute-start.5) | collective-permute-done | bytes 442400 | tf_op jit(solution)/shard_map/ppermute | solution.py:18
  432.5 2.3 copy.375
  434.8 3.4 copy.374
  438.3 6.5 %pad_maximum_fusion = f32[9,16,48,160]{3,1,2,0:T(8,128)S(1)} fusion(f32[9,16,48,16]{3,1,2,0:T(8,128)S(1)} %copy.375, f32[9,16,16,128]{3,1,2,0:T(8,128)} %copy-done.2, f32[9,16,16,128]{3,1,2,0:T(8,128)} %copy-done.1, f32[9,16,16,128]{3,1,2,0:T(8,128)} %copy-done.3, f32[9,16,48,16]{3,1,2,0:T(8,128)} %copy.374), kind=kLoop, calls=%fused_computation.15 | loop fusion | flops 4423680 | bytes 8847360 | tf_op jit(solution)/shard_map/concatenate | solution.py:19
  444.8 7.4 %fusion = f32[16,9,16,160]{3,0,2,1:T(8,128)S(1)} fusion(f32[9,16,48,160]{3,1,2,0:T(8,128)S(1)} %pad_maximum_fusion, f32[48,16]{1,0:T(8,128)S(1)} %copy-done.5), kind=kOutput, calls=%fused_computation.16 | convolution fusion | flops 212340480 | bytes 5901312 | tf_op jit(solution)/shard_map/czpy,pq->czqy/dot_general | solution.py:40
  455.6 9.0 %copy.378 = f32[6,32768]{0,1:T(8,128)} copy(f32[6,32768]{1,0:T(8,128)S(1)} %stack.327) | data formatting | bytes 1572864 | tf_op jit(solution)/shard_map/stack | solution.py:87
  464.7 16.5 %gather_fusion.11 = f32[4096,6]{1,0:T(8,128)S(1)} fusion(f32[6,32768]{0,1:T(8,128)} %copy.378, s32[4096]{0:T(1024)S(1)} %copy-done.16), kind=kCustom, calls=%fused_computation.7.clone | custom fusion | bytes 212992 | tf_op jit(solution)/shard_map/jit(_take)/gather | solution.py:59
  481.8 16.6 %gather_fusion.10 = f32[4096,6]{1,0:T(8,128)S(1)} fusion(f32[6,32768]{0,1:T(8,128)} %copy.378, s32[4096]{0:T(1024)S(1)} %copy-done.15), kind=kCustom, calls=%fused_computation.6.clone | custom fusion | bytes 212992 | tf_op jit(solution)/shard_map/jit(_take)/gather | solution.py:59
  499.0 16.8 %gather_fusion.9 = f32[4096,6]{1,0:T(8,128)S(1)} fusion(f32[6,32768]{0,1:T(8,128)} %copy.378, s32[4096]{0:T(1024)S(1)} %copy-done.14), kind=kCustom, calls=%fused_computation.5.clone | custom fusion | bytes 212992 | tf_op jit(solution)/shard_map/jit(_take)/gather | solution.py:59
  516.4 16.6 %gather_fusion.8 = f32[4096,6]{1,0:T(8,128)S(1)} fusion(f32[6,32768]{0,1:T(8,128)} %copy.378, s32[4096]{0:T(1024)S(1)} %copy-done.13), kind=kCustom, calls=%fused_computation.4.clone | custom fusion | bytes 212992 | tf_op jit(solution)/shard_map/jit(_take)/gather | solution.py:59
  533.6 16.6 %gather_fusion.7 = f32[4096,6]{1,0:T(8,128)S(1)} fusion(f32[6,32768]{0,1:T(8,128)} %copy.378, s32[4096]{0:T(1024)S(1)} %copy-done.12), kind=kCustom, calls=%fused_computation.3.clone | custom fusion | bytes 212992 | tf_op jit(solution)/shard_map/jit(_take)/gather | solution.py:59
  550.8 16.6 %gather_fusion.6 = f32[4096,6]{1,0:T(8,128)S(1)} fusion(f32[6,32768]{0,1:T(8,128)} %copy.378, s32[4096]{0:T(1024)S(1)} %copy-done.11), kind=kCustom, calls=%fused_computation.2.clone | custom fusion | bytes 212992 | tf_op jit(solution)/shard_map/jit(_take)/gather | solution.py:59
  568.0 16.6 %gather_fusion.5 = f32[4096,6]{1,0:T(8,128)S(1)} fusion(f32[6,32768]{0,1:T(8,128)} %copy.378, s32[4096]{0:T(1024)S(1)} %copy-done.10), kind=kCustom, calls=%fused_computation.1.clone | custom fusion | bytes 212992 | tf_op jit(solution)/shard_map/jit(_take)/gather | solution.py:59
  585.3 16.5 %gather_fusion.4 = f32[4096,6]{1,0:T(8,128)S(1)} fusion(f32[6,32768]{0,1:T(8,128)} %copy.378, s32[4096]{0:T(1024)S(1)} %copy-done.9), kind=kCustom, calls=%fused_computation.clone | custom fusion | bytes 212992 | tf_op jit(solution)/shard_map/jit(_take)/gather | solution.py:59
  603.8 11.0 %all-to-all-start.2 = ((f32[64,1,384]{2,1,0:T(1,128)}), f32[64,1,384]{2,1,0:T(1,128)S(1)}, u32[]{:S(2)}, u32[]{:S(2)}) async-start(f32[64,1,384]{2,1,0:T(1,128)} %reshape.704), calls=%async_computation.2 | async-start | bytes 196608 | tf_op jit(solution)/shard_map/all_to_all | solution.py:137
  614.8 10.6 %all-to-all-done.2 = f32[64,1,384]{2,1,0:T(1,128)S(1)} async-done(((f32[64,1,384]{2,1,0:T(1,128)}), f32[64,1,384]{2,1,0:T(1,128)S(1)}, u32[]{:S(2)}, u32[]{:S(2)}) %all-to-all-start.2) | async-done | bytes 98336 | tf_op jit(solution)/shard_map/all_to_all | solution.py:137
  627.1 2.8 gather_fusion.3
  (294 shorter events, 124.8 us)
Async XLA Ops:
  1.1 167.5 %collective-permute-start = (f32[3,16,16,128]{3,1,2,0:T(8,128)S(1)}, f32[3,16,16,128]{3,1,2,0:T(8,128)}, u32[]{:S(2)}, u32[]{:S(2)}) collective-permute-start(f32[3,16,16,128]{3,1,2,0:T(8,128)S(1)} %copy.360), channel_id=1, source_target_pairs={{0,1},{1,2},{2,3},{3,0},{4,5},{5,6},{6,7},{7,4},{8,9},{9,10},{10,1... | collective-permute-start | bytes 1179656 | tf_op jit(solution)/shard_map/ppermute | solution.py:17
  3.3 166.5 %collective-permute-start.1 = (f32[3,16,16,128]{3,1,2,0:T(8,128)S(1)}, f32[3,16,16,128]{3,1,2,0:T(8,128)S(1)}, u32[]{:S(2)}, u32[]{:S(2)}) collective-permute-start(f32[3,16,16,128]{3,1,2,0:T(8,128)S(1)} %copy.360), channel_id=1, source_target_pairs={{1,0},{2,1},{3,2},{0,3},{5,4},{6,5},{7,6},{4,7},{9,8},{10,9},{11,1... | collective-permute-start | bytes 1179656 | tf_op jit(solution)/shard_map/ppermute | solution.py:18
  14.0 50.2 %copy-start.36 = (s32[1024]{0:T(1024)S(1)}, s32[1024]{0:T(1024)}, u32[]{:S(2)}) copy-start(s32[1024]{0:T(1024)} %param.11) | copy-start | bytes 12292
  14.0 50.2 %copy-start.37 = (s32[1024]{0:T(1024)S(1)}, s32[1024]{0:T(1024)}, u32[]{:S(2)}) copy-start(s32[1024]{0:T(1024)} %param.10) | copy-start | bytes 12292
  14.1 50.2 %copy-start.38 = (s32[1024]{0:T(1024)S(1)}, s32[1024]{0:T(1024)}, u32[]{:S(2)}) copy-start(s32[1024]{0:T(1024)} %param.12) | copy-start | bytes 12292
  14.1 68.0 %copy-start.32 = (f32[3,1024]{1,0:T(4,128)S(1)}, f32[3,1024]{1,0:T(4,128)}, u32[]{:S(2)}) copy-start(f32[3,1024]{1,0:T(4,128)} %param.13) | copy-start | bytes 36868
  64.2 23.0 %copy-start.33 = (s32[1024]{0:T(1024)}, s32[1024]{0:T(1024)S(1)}, u32[]{:S(2)}) copy-start(s32[1024]{0:T(1024)S(1)} %get-tuple-element.69) | copy-start | bytes 12292
  69.3 323.4 %all-to-all-start.1 = ((s32[1,64,64]{2,0,1:T(1,128)}), s32[1,64,64]{2,0,1:T(1,128)}, u32[]{:S(2)}, u32[]{:S(2)}) async-start(s32[1,64,64]{2,0,1:T(1,128)} %reshape.235), calls=%async_computation.1 | async-start | bytes 65536 | tf_op jit(solution)/shard_map/all_to_all | solution.py:114
  173.1 234.5 %copy-start.1 = (f32[9,16,16,128]{3,1,2,0:T(8,128)}, f32[9,16,16,128]{3,1,2,0:T(8,128)S(1)}, u32[]{:S(2)}) copy-start(f32[9,16,16,128]{3,1,2,0:T(8,128)S(1)} %fusion.4) | copy-start | bytes 3538948
  173.1 234.5 %collective-permute-start.3 = (f32[9,16,16,128]{3,1,2,0:T(8,128)S(1)}, f32[9,16,16,128]{3,1,2,0:T(8,128)S(1)}, u32[]{:S(2)}, u32[]{:S(2)}) collective-permute-start(f32[9,16,16,128]{3,1,2,0:T(8,128)S(1)} %fusion.4), channel_id=1, source_target_pairs={{32,0},{64,32},{96,64},{128,96},{160,128},{192,160},{224,192},{0,2... | collective-permute-start | bytes 3538952 | tf_op jit(solution)/shard_map/ppermute | solution.py:18
  176.0 231.6 %collective-permute-start.2 = (f32[9,16,16,128]{3,1,2,0:T(8,128)S(1)}, f32[9,16,16,128]{3,1,2,0:T(8,128)S(1)}, u32[]{:S(2)}, u32[]{:S(2)}) collective-permute-start(f32[9,16,16,128]{3,1,2,0:T(8,128)S(1)} %fusion.4), channel_id=1, source_target_pairs={{0,32},{32,64},{64,96},{96,128},{128,160},{160,192},{192,224},{224... | collective-permute-start | bytes 3538952 | tf_op jit(solution)/shard_map/ppermute | solution.py:17
  392.6 28.1 %all-to-all-start = ((f32[64,1,192]{2,1,0:T(1,128)}), f32[64,1,192]{2,1,0:T(1,128)}, u32[]{:S(2)}, u32[]{:S(2)}) async-start(f32[64,1,192]{2,1,0:T(1,128)} %reshape.702), calls=%async_computation | async-start | bytes 131072 | tf_op jit(solution)/shard_map/all_to_all | solution.py:122
  416.2 16.2 %collective-permute-start.5 = (f32[9,16,48,16]{2,3,1,0:T(8,128)}, f32[9,16,48,16]{2,3,1,0:T(8,128)}, u32[]{:S(2)}, u32[]{:S(2)}) collective-permute-start(f32[9,16,48,16]{2,3,1,0:T(8,128)} %copy.373), channel_id=1, source_target_pairs={{4,0},{8,4},{12,8},{16,12},{20,16},{24,20},{28,24},{0,28},{5,1},{9... | collective-permute-start | bytes 1327112 | tf_op jit(solution)/shard_map/ppermute | solution.py:18
  418.9 15.9 %collective-permute-start.4 = (f32[9,16,48,16]{2,3,1,0:T(8,128)}, f32[9,16,48,16]{2,3,1,0:T(8,128)}, u32[]{:S(2)}, u32[]{:S(2)}) collective-permute-start(f32[9,16,48,16]{2,3,1,0:T(8,128)} %copy.372), channel_id=1, source_target_pairs={{0,4},{4,8},{8,12},{12,16},{16,20},{20,24},{24,28},{28,0},{1,5},{5... | collective-permute-start | bytes 1327112 | tf_op jit(solution)/shard_map/ppermute | solution.py:17
  499.0 17.4 %copy-start.13 = (s32[4096]{0:T(1024)S(1)}, s32[4096]{0:T(1024)}, u32[]{:S(2)}) copy-start(s32[4096]{0:T(1024)} %get-tuple-element.162) | copy-start | bytes 49156
  585.2 17.3 %copy-start.17 = (f32[4096]{0:T(1024)S(1)}, f32[4096]{0:T(1024)}, u32[]{:S(2)}) copy-start(f32[4096]{0:T(1024)} %get-tuple-element.145) | copy-start | bytes 49156
  585.2 17.3 %copy-start.18 = (f32[4096]{0:T(1024)S(1)}, f32[4096]{0:T(1024)}, u32[]{:S(2)}) copy-start(f32[4096]{0:T(1024)} %get-tuple-element.146) | copy-start | bytes 49156
  585.2 17.3 %copy-start.19 = (f32[4096]{0:T(1024)S(1)}, f32[4096]{0:T(1024)}, u32[]{:S(2)}) copy-start(f32[4096]{0:T(1024)} %get-tuple-element.147) | copy-start | bytes 49156
  585.2 17.3 %copy-start.20 = (f32[4096]{0:T(1024)S(1)}, f32[4096]{0:T(1024)}, u32[]{:S(2)}) copy-start(f32[4096]{0:T(1024)} %get-tuple-element.148) | copy-start | bytes 49156
  585.2 17.3 %copy-start.21 = (f32[4096]{0:T(1024)S(1)}, f32[4096]{0:T(1024)}, u32[]{:S(2)}) copy-start(f32[4096]{0:T(1024)} %get-tuple-element.149) | copy-start | bytes 49156
  585.2 17.3 %copy-start.22 = (f32[4096]{0:T(1024)S(1)}, f32[4096]{0:T(1024)}, u32[]{:S(2)}) copy-start(f32[4096]{0:T(1024)} %get-tuple-element.150) | copy-start | bytes 49156
  585.2 17.3 %copy-start.23 = (f32[4096]{0:T(1024)S(1)}, f32[4096]{0:T(1024)}, u32[]{:S(2)}) copy-start(f32[4096]{0:T(1024)} %get-tuple-element.151) | copy-start | bytes 49156
  585.2 17.3 %copy-start.24 = (pred[4096]{0:T(1024)(128)(4,1)S(1)}, pred[4096]{0:T(1024)(128)(4,1)}, u32[]{:S(2)}) copy-start(pred[4096]{0:T(1024)(128)(4,1)} %get-tuple-element.152) | copy-start | bytes 12292
  585.2 17.3 %copy-start.25 = (pred[4096]{0:T(1024)(128)(4,1)S(1)}, pred[4096]{0:T(1024)(128)(4,1)}, u32[]{:S(2)}) copy-start(pred[4096]{0:T(1024)(128)(4,1)} %get-tuple-element.153) | copy-start | bytes 12292
  585.2 17.3 %copy-start.26 = (pred[4096]{0:T(1024)(128)(4,1)S(1)}, pred[4096]{0:T(1024)(128)(4,1)}, u32[]{:S(2)}) copy-start(pred[4096]{0:T(1024)(128)(4,1)} %get-tuple-element.154) | copy-start | bytes 12292
  585.2 17.3 %copy-start.27 = (pred[4096]{0:T(1024)(128)(4,1)S(1)}, pred[4096]{0:T(1024)(128)(4,1)}, u32[]{:S(2)}) copy-start(pred[4096]{0:T(1024)(128)(4,1)} %get-tuple-element.155) | copy-start | bytes 12292
  585.2 17.3 %copy-start.28 = (pred[4096]{0:T(1024)(128)(4,1)S(1)}, pred[4096]{0:T(1024)(128)(4,1)}, u32[]{:S(2)}) copy-start(pred[4096]{0:T(1024)(128)(4,1)} %get-tuple-element.156) | copy-start | bytes 12292
  585.3 17.3 %copy-start.29 = (pred[4096]{0:T(1024)(128)(4,1)S(1)}, pred[4096]{0:T(1024)(128)(4,1)}, u32[]{:S(2)}) copy-start(pred[4096]{0:T(1024)(128)(4,1)} %get-tuple-element.157) | copy-start | bytes 12292
  585.3 17.3 %copy-start.30 = (pred[4096]{0:T(1024)(128)(4,1)S(1)}, pred[4096]{0:T(1024)(128)(4,1)}, u32[]{:S(2)}) copy-start(pred[4096]{0:T(1024)(128)(4,1)} %get-tuple-element.158) | copy-start | bytes 12292
  585.3 17.3 %copy-start.31 = (pred[4096]{0:T(1024)(128)(4,1)S(1)}, pred[4096]{0:T(1024)(128)(4,1)}, u32[]{:S(2)}) copy-start(pred[4096]{0:T(1024)(128)(4,1)} %get-tuple-element.159) | copy-start | bytes 12292
  602.9 27.0 %copy-start.35 = (pred[1024]{0:T(1024)(128)(4,1)S(1)}, pred[1024]{0:T(1024)(128)(4,1)}, u32[]{:S(2)}) copy-start(pred[1024]{0:T(1024)(128)(4,1)} %get-tuple-element.68) | copy-start | bytes 3076
  603.8 21.6 %all-to-all-start.2 = ((f32[64,1,384]{2,1,0:T(1,128)}), f32[64,1,384]{2,1,0:T(1,128)S(1)}, u32[]{:S(2)}, u32[]{:S(2)}) async-start(f32[64,1,384]{2,1,0:T(1,128)} %reshape.704), calls=%async_computation.2 | async-start | bytes 196608 | tf_op jit(solution)/shard_map/all_to_all | solution.py:137
  (16 other events, 169.2 us)
